TPU v7x, 256 devices: a whole 4x4x8 slice. The times are simulated.
256 devices in a mesh: ent: 64 (over z, y, core), rel: 4 (over x).
Axes of the slice: x: 4, y: 4, z: 8, core: 2. Of those that a mesh axis runs over, the one named last changes fastest.
Arguments:
- entity_rows: bfloat16 [65536, 256], P('ent'), may hold values from -2.5 to 2.5
- request_rows: int32 [64, 64, 32], P('ent'), may hold values from 0 to 1023
- edge_heads: int32 [262144], P(('ent', 'rel')), may hold values from 0 to 1023
- edge_rels: int32 [262144], P(('ent', 'rel')), may hold values from 0 to 7
- edge_tails: int32 [262144], P(('ent', 'rel')), may hold values from 0 to 2047
- edge_counts: int32 [256], P(('ent', 'rel')), may hold values from 1 to 1024, 163840 in all
- negative_rows: int32 [65536], P(('ent', 'rel')), may hold values from 0 to 1023
- relation_blocks: bfloat16 [32, 8, 32, 32], P('rel'), may hold values from -1 to 1
Outputs:
- entity_grad: float32 [65536, 256], P('ent')
- relation_grad: float32 [32, 8, 32, 32], P('rel')
Inputs may be any that keep to these rules, and one draw needn't show every extreme that they name: Edge slots of bucket b at or past edge_counts[b] are ignored; some bucket is full in every draw.
All inputs are finite; a program needn't handle non-finite values. No bound on the sum of `edge_counts` on one device may be relied on, other than what follows from the above.
Results may differ from a plain program's by a relative error of at most 0.009.
Values may be sent and summed in bfloat16 or wider, within the bound.
No kernel may reach another device: no remote copies, remote signals or barrier semaphores. Data moves between devices by JAX's collectives and lax.ppermute only.
A program may use at most 64 MiB of HBM per device.

v0:
```python
import math
import jax
import jax.numpy as jnp
from jax import lax
from jax.sharding import PartitionSpec as P


def pick_rows(indices, source_table):
    row_total = indices.shape[0]
    block_size = math.gcd(row_total, 256)
    grouped = indices.reshape(row_total // block_size, block_size)
    columns = jnp.arange(source_table.shape[0], dtype=jnp.int32)

    def pick_block(index_block):
        one_hot = (index_block[:, None] == columns[None, :]).astype(jnp.bfloat16)
        return jnp.dot(one_hot, source_table, preferred_element_type=jnp.float32).astype(
            jnp.bfloat16
        )

    picked = lax.map(pick_block, grouped)
    return picked.reshape(row_total, source_table.shape[1])


def owner_add(indices, gradients, entity_count):
    start_value = jnp.zeros((entity_count, gradients.shape[1]), jnp.float32)
    return start_value.at[indices].add(gradients)


def local(
    entity_rows,
    request_rows,
    edge_heads,
    edge_rels,
    edge_tails,
    edge_counts,
    negative_rows,
    relation_blocks,
):
    entity_count, feature_width = entity_rows.shape
    part_count = request_rows.shape[1]
    slot_count = request_rows.shape[2]
    r_count, block_count, block_width = (
        relation_blocks.shape[0],
        relation_blocks.shape[1],
        relation_blocks.shape[2],
    )
    neg_count = negative_rows.shape[0]
    owner_lists = lax.all_to_all(request_rows, "ent", split_axis=1, concat_axis=0, tiled=True)
    wanted = pick_rows(owner_lists.reshape(-1), entity_rows).reshape(
        part_count, 1, slot_count, feature_width
    )
    fetched = lax.all_to_all(wanted, "ent", split_axis=0, concat_axis=1, tiled=True)
    fetched = fetched.reshape(part_count * slot_count, feature_width)
    neg_rows = pick_rows(negative_rows, entity_rows)
    edge_dev = edge_heads.shape[0]
    block_size = math.gcd(edge_dev, 256)
    block_total = edge_dev // block_size
    live_count = edge_counts[0]
    positions = jnp.arange(edge_dev, dtype=jnp.int32).reshape(block_total, block_size)
    entity_columns = jnp.arange(entity_count, dtype=jnp.int32)
    slot_columns = jnp.arange(part_count * slot_count, dtype=jnp.int32)
    rel_columns = jnp.arange(r_count, dtype=jnp.int32)
    contract_rows = (((0,), (0,)), ((), ()))

    def edge_block(running, block_inputs):
        slot_acc, entity_acc, neg_acc, relation_acc = running
        head_ids, rel_ids, tail_ids, places = block_inputs
        live_mask = (places < live_count).astype(jnp.float32)
        head_hot = (head_ids[:, None] == entity_columns[None, :]).astype(jnp.bfloat16)
        tail_hot = (tail_ids[:, None] == slot_columns[None, :]).astype(jnp.bfloat16)
        head_rows = jnp.dot(head_hot, entity_rows, preferred_element_type=jnp.float32).astype(
            jnp.bfloat16
        )
        tail_rows = jnp.dot(tail_hot, fetched, preferred_element_type=jnp.float32).astype(
            jnp.bfloat16
        )
        rel_hot = (rel_ids[:, None] == rel_columns[None, :]).astype(jnp.float32)
        head_split = head_rows.reshape(block_size, block_count, block_width)
        proj_all = jnp.einsum(
            "enb,rnbc->renc", head_split, relation_blocks, preferred_element_type=jnp.float32
        )
        projected = (
            jnp.sum(rel_hot.T[:, :, None, None] * proj_all, 0)
            .reshape(block_size, feature_width)
            .astype(jnp.bfloat16)
        )
        projected_wide = projected.astype(jnp.float32)
        positive = jnp.sum(projected_wide * tail_rows.astype(jnp.float32), -1)
        negative = lax.dot_general(
            projected, neg_rows, (((1,), (1,)), ((), ())), preferred_element_type=jnp.float32
        )
        pos_weight = -live_mask * jax.nn.sigmoid(-positive)
        neg_weight = (live_mask[:, None] * jax.nn.sigmoid(negative) / neg_count).astype(
            jnp.bfloat16
        )
        grad_proj = (
            pos_weight[:, None] * tail_rows.astype(jnp.float32)
            + jnp.dot(neg_weight, neg_rows, preferred_element_type=jnp.float32)
        ).astype(jnp.bfloat16)
        weighted = (pos_weight[:, None] * projected_wide).astype(jnp.bfloat16)
        grad_split = grad_proj.reshape(block_size, block_count, block_width)
        back_all = jnp.einsum(
            "enc,rnbc->renb", grad_split, relation_blocks, preferred_element_type=jnp.float32
        )
        head_grad = (
            jnp.sum(rel_hot.T[:, :, None, None] * back_all, 0)
            .reshape(block_size, feature_width)
            .astype(jnp.bfloat16)
        )
        slot_acc = slot_acc + lax.dot_general(
            tail_hot, weighted, contract_rows, preferred_element_type=jnp.float32
        )
        entity_acc = entity_acc + lax.dot_general(
            head_hot, head_grad, contract_rows, preferred_element_type=jnp.float32
        )
        neg_acc = neg_acc + lax.dot_general(
            neg_weight, projected, contract_rows, preferred_element_type=jnp.float32
        )
        masked_heads = rel_hot.T.astype(jnp.bfloat16)[:, :, None, None] * head_split[None]
        relation_acc = relation_acc + jnp.einsum(
            "renb,enc->rnbc", masked_heads, grad_split, preferred_element_type=jnp.float32
        )
        return ((slot_acc, entity_acc, neg_acc, relation_acc), None)

    start_values = (
        jnp.zeros((part_count * slot_count, feature_width), jnp.float32),
        jnp.zeros((entity_count, feature_width), jnp.float32),
        jnp.zeros((neg_count, feature_width), jnp.float32),
        jnp.zeros(relation_blocks.shape, jnp.float32),
    )
    block_inputs = (
        edge_heads.reshape(block_total, block_size),
        edge_rels.reshape(block_total, block_size),
        edge_tails.reshape(block_total, block_size),
        positions,
    )
    (slot_acc, entity_acc, neg_acc, relation_acc), _ = lax.scan(
        edge_block, start_values, block_inputs
    )
    neg_hot = (negative_rows[:, None] == entity_columns[None, :]).astype(jnp.bfloat16)
    entity_acc = entity_acc + lax.dot_general(
        neg_hot, neg_acc.astype(jnp.bfloat16), contract_rows, preferred_element_type=jnp.float32
    )
    slot_grads = slot_acc.reshape(1, part_count, slot_count, feature_width)
    returned = lax.all_to_all(
        slot_grads.astype(jnp.bfloat16), "ent", split_axis=1, concat_axis=0, tiled=True
    ).astype(slot_grads.dtype)
    entity_acc = entity_acc + owner_add(
        owner_lists.reshape(-1), returned.reshape(-1, feature_width), entity_count
    )
    entity_grad = lax.psum(entity_acc, "rel")
    relation_grad = lax.psum(relation_acc, "ent")
    return (entity_grad, relation_grad)


def solution(mesh):
    in_specs = (
        P("ent", None),
        P("ent", None, None),
        P(("ent", "rel")),
        P(("ent", "rel")),
        P(("ent", "rel")),
        P(("ent", "rel")),
        P(("ent", "rel")),
        P("rel", None, None, None),
    )
    out_specs = (P("ent", None), P("rel", None, None, None))
    return jax.shard_map(local, mesh=mesh, in_specs=in_specs, out_specs=out_specs, check_vma=False)
```

profile of v0, /device:TPU:8, one launch (start us, length us, event | category | flops | bytes accessed | tf_op | source)
XLA Modules:
  0.0 383.0 jit_solution(16212449031649504692)
XLA Ops:
  7.2 1.4 copy.20
  8.6 12.1 %all-to-all-start = ((s32[1,64,32]{2,0,1:T(1,128)}), s32[1,64,32]{2,0,1:T(1,128)S(1)}, u32[]{:S(2)}, u32[]{:S(2)}) async-start(s32[1,64,32]{2,0,1:T(1,128)} %copy.20), calls=%async_computation | async-start | bytes 65536 | tf_op jit(solution)/shard_map/all_to_all | solution.py:48
  20.7 8.5 %all-to-all-done = s32[1,64,32]{2,0,1:T(1,128)S(1)} async-done(((s32[1,64,32]{2,0,1:T(1,128)}), s32[1,64,32]{2,0,1:T(1,128)S(1)}, u32[]{:S(2)}, u32[]{:S(2)}) %all-to-all-start) | async-done | bytes 8224 | tf_op jit(solution)/shard_map/all_to_all | solution.py:48
  29.8 0.7 reduce.5
  30.6 16.5 %while.32 = (s32[]{:T(128)}, bf16[8,256,256]{2,1,0:T(8,128)(2,1)}, s32[8,256]{1,0:T(8,128)S(1)}, bf16[1024,256]{1,0:T(8,128)(2,1)}, s32[]{:T(128)}) while((s32[]{:T(128)}, bf16[8,256,256]{2,1,0:T(8,128)(2,1)}, s32[8,256]{1,0:T(8,128)S(1)}, bf16[1024,256]{1,0:T(8,128)(2,1)}, s32[]{:T(128)}) %tuple.56), condition=%wide.region_1.2_spmd.clone, body=%wide.region_0.1_spmd.clone.sunk | while | flops 134545408 | bytes 658509 | solution.py:20
  30.6 2.1 fusion.90
  32.6 2.0 fusion.90
  34.7 2.0 fusion.90
  36.8 2.1 fusion.90
  38.8 2.1 fusion.90
  40.9 2.0 fusion.90
  42.9 2.0 fusion.90
  45.0 2.1 fusion.90
  47.0 6.5 %all-to-all-start.1 = ((bf16[64,1,32,256]{3,2,1,0:T(8,128)(2,1)}), bf16[64,1,32,256]{3,2,1,0:T(8,128)(2,1)}, u32[]{:S(2)}, u32[]{:S(2)}) async-start(bf16[64,1,32,256]{3,2,1,0:T(8,128)(2,1)} %bitcast.1), calls=%async_computation.1 | async-start | bytes 2097152 | tf_op jit(solution)/shard_map/all_to_all | solution.py:52
  53.6 1.9 copy.21
  55.5 1.4 convolution_convert_fusion.2
  56.9 25.4 %all-to-all-done.1 = bf16[64,1,32,256]{3,2,1,0:T(8,128)(2,1)} async-done(((bf16[64,1,32,256]{3,2,1,0:T(8,128)(2,1)}), bf16[64,1,32,256]{3,2,1,0:T(8,128)(2,1)}, u32[]{:S(2)}, u32[]{:S(2)}) %all-to-all-start.1) | async-done | bytes 1048608 | tf_op jit(solution)/shard_map/all_to_all | solution.py:52
  82.3 38.9 %while.33 = (s32[]{:T(128)}, f32[2048,256]{1,0:T(8,128)S(1)}, f32[1024,256]{1,0:T(8,128)S(1)}, f32[256,256]{1,0:T(8,128)S(1)}, f32[8,8,32,32]{2,3,0,1:T(8,128)},...) while((s32[]{:T(128)}, f32[2048,256]{1,0:T(8,128)S(1)}, ...), condition=%wide.region_6.7_spmd.clone, body=%wide.region_2.6_spmd.clone.sunk | while | flops 1016077568 | bytes 14733582 | solution.py:137
  83.0 1.5 convolution_convert_fusion.4
  84.5 1.5 fusion.110
  86.6 2.1 fusion.111
  89.4 0.9 fusion.115
  90.9 1.1 convolution_add_fusion.8
  92.8 1.5 convolution_convert_fusion.4
  94.3 1.5 fusion.110
  96.4 2.1 fusion.111
  99.1 0.9 fusion.115
  100.7 1.1 convolution_add_fusion.8
  102.5 1.5 convolution_convert_fusion.4
  104.0 1.5 fusion.110
  106.1 2.1 fusion.111
  108.9 0.9 fusion.115
  110.4 1.1 convolution_add_fusion.8
  112.2 1.5 convolution_convert_fusion.4
  113.7 1.5 fusion.110
  115.8 2.1 fusion.111
  118.6 0.9 fusion.115
  120.2 1.1 convolution_add_fusion.8
  121.2 1.1 convert_element_type.106
  122.3 5.9 %all-to-all-start.2 = ((bf16[1,64,32,256]{3,2,0,1:T(8,128)(2,1)}), bf16[1,64,32,256]{3,2,0,1:T(8,128)(2,1)S(1)}, u32[]{:S(2)}, u32[]{:S(2)}) async-start(bf16[1,64,32,256]{3,2,0,1:T(8,128)(2,1)} %bitcast.124), calls=%async_computation.2 | async-start | bytes 2097152 | tf_op jit(solution)/shard_map/all_to_all | solution.py:145
  128.4 1.4 copy.22
  130.4 27.4 %all-to-all-done.2 = bf16[1,64,32,256]{3,2,0,1:T(8,128)(2,1)S(1)} async-done(((bf16[1,64,32,256]{3,2,0,1:T(8,128)(2,1)}), bf16[1,64,32,256]{3,2,0,1:T(8,128)(2,1)S(1)}, u32[]{:S(2)}, u32[]{:S(2)}) %all-to-all-start.2) | async-done | bytes 1048608 | tf_op jit(solution)/shard_map/all_to_all | solution.py:145
  157.7 12.0 %scatter_custom_fusion = f32[1024,256]{1,0:T(8,128)S(1)} fusion(f32[1024,256]{1,0:T(8,128)S(1)} %convolution_add_fusion.4, s32[2048]{0:T(1024)S(1)} %bitcast.138, bf16[2048,256]{1,0:T(8,128)(2,1)S(1)} %bitcast.125), kind=kCustom, calls=%fused_computation.57 | custom fusion | flops 1048576 | bytes 2097152 | tf_op jit(solution)/shard_map/scatter-add | solution.py:26
  169.8 1.0 copy-done.3
  170.8 150.9 %all-reduce.5.cloned.1.call-done = f32[8,8,32,32]{3,2,1,0:T(8,128)} async-done(((f32[8,8,32,32]{3,2,1,0:T(8,128)}), f32[8,8,32,32]{3,2,1,0:T(8,128)}) %all-reduce.5.cloned.1.call-update) | async-done | bytes 262160 | tf_op jit(solution)/shard_map/psum | solution.py:152
  321.6 51.3 %all-reduce.3.cloned.1.call-done = f32[1024,256]{1,0:T(8,128)} async-done(((f32[1024,256]{1,0:T(8,128)}), f32[1024,256]{1,0:T(8,128)}) %all-reduce.3.cloned.1.call-update) | async-done | bytes 1048592 | tf_op jit(solution)/shard_map/psum | solution.py:151
  372.9 2.3 copy.51
  375.2 1.0 copy.52
  (107 shorter events, 11.3 us)
Async XLA Ops:
  8.6 20.7 %all-to-all-start = ((s32[1,64,32]{2,0,1:T(1,128)}), s32[1,64,32]{2,0,1:T(1,128)S(1)}, u32[]{:S(2)}, u32[]{:S(2)}) async-start(s32[1,64,32]{2,0,1:T(1,128)} %copy.20), calls=%async_computation | async-start | bytes 65536 | tf_op jit(solution)/shard_map/all_to_all | solution.py:48
  29.2 1.3 copy-start.6
  47.0 6.5 %copy-start.8 = (s32[1024]{0:T(1024)S(1)}, s32[1024]{0:T(1024)}, u32[]{:S(2)}) copy-start(s32[1024]{0:T(1024)} %param.14) | copy-start | bytes 12292
  47.0 6.5 %copy-start.9 = (s32[1024]{0:T(1024)S(1)}, s32[1024]{0:T(1024)}, u32[]{:S(2)}) copy-start(s32[1024]{0:T(1024)} %param.15) | copy-start | bytes 12292
  47.0 6.6 %copy-start.10 = (s32[1024]{0:T(1024)S(1)}, s32[1024]{0:T(1024)}, u32[]{:S(2)}) copy-start(s32[1024]{0:T(1024)} %param.16) | copy-start | bytes 12292
  47.0 35.3 %all-to-all-start.1 = ((bf16[64,1,32,256]{3,2,1,0:T(8,128)(2,1)}), bf16[64,1,32,256]{3,2,1,0:T(8,128)(2,1)}, u32[]{:S(2)}, u32[]{:S(2)}) async-start(bf16[64,1,32,256]{3,2,1,0:T(8,128)(2,1)} %bitcast.1), calls=%async_computation.1 | async-start | bytes 2097152 | tf_op jit(solution)/shard_map/all_to_all | solution.py:52
  86.4 2.6 copy-start.5
  86.6 2.8 copy-start
  90.4 1.7 copy-start.1
  96.1 2.6 copy-start.5
  96.4 2.8 copy-start
  100.1 1.7 copy-start.1
  105.8 2.6 copy-start.5
  106.1 2.8 copy-start
  109.8 1.7 copy-start.1
  115.6 2.6 copy-start.5
  115.8 2.8 copy-start
  119.6 1.7 copy-start.1
  121.2 7.0 %copy-start.7 = (s32[1,64,32]{2,0,1:T(1,128)S(1)}, s32[1,64,32]{2,0,1:T(1,128)}, u32[]{:S(2)}) copy-start(s32[1,64,32]{2,0,1:T(1,128)} %copy-done.6) | copy-start | bytes 24580
  122.3 6.0 %copy-start.2 = (f32[8,8,32,32]{2,3,0,1:T(8,128)S(1)}, f32[8,8,32,32]{2,3,0,1:T(8,128)}, u32[]{:S(2)}) copy-start(f32[8,8,32,32]{2,3,0,1:T(8,128)} %get-tuple-element.138) | copy-start | bytes 786436
  122.3 35.4 %all-to-all-start.2 = ((bf16[1,64,32,256]{3,2,0,1:T(8,128)(2,1)}), bf16[1,64,32,256]{3,2,0,1:T(8,128)(2,1)S(1)}, u32[]{:S(2)}, u32[]{:S(2)}) async-start(bf16[1,64,32,256]{3,2,0,1:T(8,128)(2,1)} %bitcast.124), calls=%async_computation.2 | async-start | bytes 2097152 | tf_op jit(solution)/shard_map/all_to_all | solution.py:145
  128.2 1.6 copy-start.11
  128.2 193.4 %all-reduce.5.cloned.1.call-start = ((), (), s32[]{:S(2)}) async-start(), calls=%async_computation.4 | async-start | bytes 2097152 | tf_op jit(solution)/shard_map/psum | solution.py:152
  129.8 243.2 %all-reduce.3.cloned.1.call-start = ((), (), s32[]{:S(2)}) async-start(), calls=%async_computation.3 | async-start | bytes 2097152 | tf_op jit(solution)/shard_map/psum | solution.py:151
  169.8 1.0 copy-start.3
  321.6 53.6 %copy-start.4 = (f32[8,8,32,32]{3,2,1,0:T(8,128)S(1)}, f32[8,8,32,32]{3,2,1,0:T(8,128)}, u32[]{:S(2)}) copy-start(f32[8,8,32,32]{3,2,1,0:T(8,128)} %all-reduce.5.cloned.1.call-done) | copy-start | bytes 786436
Sparse Core Ops, SparseCore 0:
  132.4 189.1 all-reduce.4
  324.6 48.3 all-reduce.2
where the time goes:
time: 384 us; the launch traced here: 383 us
  waiting for transfers between devices  263 us (68%)
  matrix products  53.8 us (14%)
  starting transfers between devices  24.5 us (6%)
  other arithmetic  16.5 us (4%)
  between operations  14.2 us (4%)
  local copies, waits for them, and re-layouts  9.81 us (3%)
    psum x1, waiting for transfers between devices, local(): relation_grad = lax.psum(relation_acc, 'ent')  151 us
    psum x1, waiting for transfers between devices, local(): entity_grad = lax.psum(entity_acc, 'rel')  51.3 us
    all_to_all x1, waiting for transfers between devices, local(): lax.all_to_all(slot_grads.astype(jnp.bfloat16), 'ent', split_axis=1, conc...  27.4 us
    all_to_all x1, waiting for transfers between devices, local(): lax.all_to_all(wanted, 'ent', split_axis=0, concat_axis=1, tiled=True)  25.4 us
    dot_general x9, matrix products, pick_block(): jnp.dot(one_hot, source_table, preferred_element_type=jnp.float32)  17.8 us
    all_to_all x1, starting transfers between devices, local(): lax.all_to_all(request_rows, 'ent', split_axis=1, concat_axis=0, tiled=True)  12.1 us
    scatter-add x1, other arithmetic, owner_add(): return start_value.at[indices].add(gradients)  12 us
    all_to_all x1, waiting for transfers between devices, local(): lax.all_to_all(request_rows, 'ent', split_axis=1, concat_axis=0, tiled=True)  8.54 us
  transfers between devices with their start and end apart: 5, of which 5 were waited for; matrix products, arithmetic and copies ran while one was open for 5% of the time, Pallas kernels for 0%

commit v1 on v0

--- a/solution.py
+++ b/solution.py
@@ -148,7 +148,11 @@
     entity_acc = entity_acc + owner_add(
         owner_lists.reshape(-1), returned.reshape(-1, feature_width), entity_count
     )
-    entity_grad = lax.psum(entity_acc, "rel")
+    entity_grad = entity_acc
+    for hop in (1, 2):
+        entity_grad = entity_grad + lax.ppermute(
+            entity_grad, "rel", [(dev, dev ^ hop) for dev in range(4)]
+        )
     relation_grad = lax.psum(relation_acc, "ent")
     return (entity_grad, relation_grad)
 

time: 384 us -> 392 us (1.021)
  starting transfers between devices: 24.5 us -> 29.2 us
    psum x1 -> x0, waiting for transfers between devices: 51.3 us -> none  [local(): entity_grad = lax.psum(entity_acc, 'rel')]
    ppermute x0 -> x2, waiting for transfers between devices: none -> 42.7 us  [local(): lax.ppermute(entity_grad, 'rel', [(dev, dev ^ hop) for dev in range(4)])]
    psum x1, waiting for transfers between devices: 151 us -> 162 us  [local(): relation_grad = lax.psum(relation_acc, 'ent')]
    ppermute x0 -> x2, starting transfers between devices: none -> 4.68 us  [local(): lax.ppermute(entity_grad, 'rel', [(dev, dev ^ hop) for dev in range(4)])]
  transfers between devices with their start and end apart: 5 -> 6, of which waited for: 5 -> 6; matrix products, arithmetic and copies ran while one was open for 5% -> 2% of each run, Pallas kernels for 0% -> 0%
where the time goes in v1:
time: 392 us; the launch traced here: 390 us
  waiting for transfers between devices  266 us (68%)
  matrix products  53.8 us (14%)
  starting transfers between devices  29.2 us (7%)
  other arithmetic  18.2 us (5%)
  between operations  14.2 us (4%)
  local copies, waits for them, and re-layouts  7.81 us (2%)
    psum x1, waiting for transfers between devices, local(): relation_grad = lax.psum(relation_acc, 'ent')  162 us
    ppermute x2, waiting for transfers between devices, local(): lax.ppermute(entity_grad, 'rel', [(dev, dev ^ hop) for dev in range(4)])  42.7 us
    all_to_all x1, waiting for transfers between devices, local(): lax.all_to_all(slot_grads.astype(jnp.bfloat16), 'ent', split_axis=1, conc...  27.9 us
    all_to_all x1, waiting for transfers between devices, local(): lax.all_to_all(wanted, 'ent', split_axis=0, concat_axis=1, tiled=True)  25.4 us
    dot_general x9, matrix products, pick_block(): jnp.dot(one_hot, source_table, preferred_element_type=jnp.float32)  17.8 us
    scatter-add x1, other arithmetic, owner_add(): return start_value.at[indices].add(gradients)  12.4 us
    all_to_all x1, starting transfers between devices, local(): lax.all_to_all(request_rows, 'ent', split_axis=1, concat_axis=0, tiled=True)  12.1 us
    all_to_all x1, waiting for transfers between devices, local(): lax.all_to_all(request_rows, 'ent', split_axis=1, concat_axis=0, tiled=True)  8.54 us
  transfers between devices with their start and end apart: 6, of which 6 were waited for; matrix products, arithmetic and copies ran while one was open for 2% of the time, Pallas kernels for 0%

profile of v1, /device:TPU:8, one launch (start us, length us, event | category | flops | bytes accessed | tf_op | source)
XLA Modules:
  0.0 390.3 jit_solution(5676655966950386531)
XLA Ops:
  7.2 1.4 copy.20
  8.6 12.1 %all-to-all-start = ((s32[1,64,32]{2,0,1:T(1,128)}), s32[1,64,32]{2,0,1:T(1,128)S(1)}, u32[]{:S(2)}, u32[]{:S(2)}) async-start(s32[1,64,32]{2,0,1:T(1,128)} %copy.20), calls=%async_computation | async-start | bytes 65536 | tf_op jit(solution)/shard_map/all_to_all | solution.py:48
  20.7 8.5 %all-to-all-done = s32[1,64,32]{2,0,1:T(1,128)S(1)} async-done(((s32[1,64,32]{2,0,1:T(1,128)}), s32[1,64,32]{2,0,1:T(1,128)S(1)}, u32[]{:S(2)}, u32[]{:S(2)}) %all-to-all-start) | async-done | bytes 8224 | tf_op jit(solution)/shard_map/all_to_all | solution.py:48
  30.6 16.5 %while.32 = (s32[]{:T(128)}, bf16[8,256,256]{2,1,0:T(8,128)(2,1)}, s32[8,256]{1,0:T(8,128)S(1)}, bf16[1024,256]{1,0:T(8,128)(2,1)}, s32[]{:T(128)}) while((s32[]{:T(128)}, bf16[8,256,256]{2,1,0:T(8,128)(2,1)}, s32[8,256]{1,0:T(8,128)S(1)}, bf16[1024,256]{1,0:T(8,128)(2,1)}, s32[]{:T(128)}) %tuple.56), condition=%wide.region_1.2_spmd.clone, body=%wide.region_0.1_spmd.clone.sunk | while | flops 134545408 | bytes 658509 | solution.py:20
  30.6 2.1 fusion.90
  32.6 2.0 fusion.90
  34.7 2.0 fusion.90
  36.8 2.1 fusion.90
  38.8 2.1 fusion.90
  40.9 2.0 fusion.90
  42.9 2.0 fusion.90
  45.0 2.1 fusion.90
  47.0 6.5 %all-to-all-start.1 = ((bf16[64,1,32,256]{3,2,1,0:T(8,128)(2,1)}), bf16[64,1,32,256]{3,2,1,0:T(8,128)(2,1)}, u32[]{:S(2)}, u32[]{:S(2)}) async-start(bf16[64,1,32,256]{3,2,1,0:T(8,128)(2,1)} %bitcast.1), calls=%async_computation.1 | async-start | bytes 2097152 | tf_op jit(solution)/shard_map/all_to_all | solution.py:52
  53.6 1.9 copy.21
  55.5 1.4 convolution_convert_fusion.2
  56.9 25.4 %all-to-all-done.1 = bf16[64,1,32,256]{3,2,1,0:T(8,128)(2,1)} async-done(((bf16[64,1,32,256]{3,2,1,0:T(8,128)(2,1)}), bf16[64,1,32,256]{3,2,1,0:T(8,128)(2,1)}, u32[]{:S(2)}, u32[]{:S(2)}) %all-to-all-start.1) | async-done | bytes 1048608 | tf_op jit(solution)/shard_map/all_to_all | solution.py:52
  82.3 38.9 %while.33 = (s32[]{:T(128)}, f32[2048,256]{1,0:T(8,128)S(1)}, f32[1024,256]{1,0:T(8,128)S(1)}, f32[256,256]{1,0:T(8,128)S(1)}, f32[8,8,32,32]{2,3,0,1:T(8,128)},...) while((s32[]{:T(128)}, f32[2048,256]{1,0:T(8,128)S(1)}, ...), condition=%wide.region_6.7_spmd.clone, body=%wide.region_2.6_spmd.clone.sunk | while | flops 1016077568 | bytes 14733582 | solution.py:137
  83.0 1.5 convolution_convert_fusion.4
  84.5 1.5 fusion.110
  86.6 2.1 fusion.111
  89.4 0.9 fusion.115
  90.9 1.1 convolution_add_fusion.8
  92.8 1.5 convolution_convert_fusion.4
  94.3 1.5 fusion.110
  96.4 2.1 fusion.111
  99.1 0.9 fusion.115
  100.7 1.1 convolution_add_fusion.8
  102.5 1.5 convolution_convert_fusion.4
  104.0 1.5 fusion.110
  106.1 2.1 fusion.111
  108.9 0.9 fusion.115
  110.4 1.1 convolution_add_fusion.8
  112.2 1.5 convolution_convert_fusion.4
  113.7 1.5 fusion.110
  115.8 2.1 fusion.111
  120.2 1.1 convolution_add_fusion.8
  121.3 1.1 convert_element_type.106
  122.3 5.9 %all-to-all-start.2 = ((bf16[1,64,32,256]{3,2,0,1:T(8,128)(2,1)}), bf16[1,64,32,256]{3,2,0,1:T(8,128)(2,1)}, u32[]{:S(2)}, u32[]{:S(2)}) async-start(bf16[1,64,32,256]{3,2,0,1:T(8,128)(2,1)} %bitcast.124), calls=%async_computation.2 | async-start | bytes 2097152 | tf_op jit(solution)/shard_map/all_to_all | solution.py:145
  129.0 27.9 %all-to-all-done.2 = bf16[1,64,32,256]{3,2,0,1:T(8,128)(2,1)} async-done(((bf16[1,64,32,256]{3,2,0,1:T(8,128)(2,1)}), bf16[1,64,32,256]{3,2,0,1:T(8,128)(2,1)}, u32[]{:S(2)}, u32[]{:S(2)}) %all-to-all-start.2) | async-done | bytes 1048608 | tf_op jit(solution)/shard_map/all_to_all | solution.py:145
  156.9 12.4 %scatter_custom_fusion = f32[1024,256]{1,0:T(8,128)S(1)} fusion(f32[1024,256]{1,0:T(8,128)S(1)} %convolution_add_fusion.4, s32[2048]{0:T(1024)S(1)} %bitcast.137, bf16[2048,256]{1,0:T(8,128)(2,1)} %bitcast.25), kind=kCustom, calls=%fused_computation.57 | custom fusion | flops 1048576 | bytes 2097152 | tf_op jit(solution)/shard_map/scatter-add | solution.py:26
  169.4 1.6 collective-permute-start
  171.0 22.4 %collective-permute-done = f32[1024,256]{1,0:T(8,128)S(1)} collective-permute-done((f32[1024,256]{1,0:T(8,128)S(1)}, f32[1024,256]{1,0:T(8,128)S(1)}, u32[]{:S(2)}, u32[]{:S(2)}) %collective-permute-start) | collective-permute-done | bytes 1048608 | tf_op jit(solution)/shard_map/ppermute | solution.py:153
  193.5 3.1 collective-permute-start.1
  196.6 1.3 copy.22
  198.0 20.2 %collective-permute-done.1 = f32[1024,256]{1,0:T(8,128)S(1)} collective-permute-done((f32[1024,256]{1,0:T(8,128)S(1)}, f32[1024,256]{1,0:T(8,128)S(1)}, u32[]{:S(2)}, u32[]{:S(2)}) %collective-permute-start.1) | collective-permute-done | bytes 1048608 | tf_op jit(solution)/shard_map/ppermute | solution.py:153
  218.2 1.1 add.66
  219.3 161.9 %all-reduce.2.cloned.1.call-done = f32[8,8,32,32]{3,2,1,0:T(8,128)} async-done(((f32[8,8,32,32]{3,2,1,0:T(8,128)}), f32[8,8,32,32]{3,2,1,0:T(8,128)}) %all-reduce.2.cloned.1.call-update) | async-done | bytes 262160 | tf_op jit(solution)/shard_map/psum | solution.py:156
  381.2 2.3 copy.50
  (105 shorter events, 13.0 us)
Async XLA Ops:
  8.6 20.7 %all-to-all-start = ((s32[1,64,32]{2,0,1:T(1,128)}), s32[1,64,32]{2,0,1:T(1,128)S(1)}, u32[]{:S(2)}, u32[]{:S(2)}) async-start(s32[1,64,32]{2,0,1:T(1,128)} %copy.20), calls=%async_computation | async-start | bytes 65536 | tf_op jit(solution)/shard_map/all_to_all | solution.py:48
  29.2 1.3 copy-start.4
  47.0 6.5 %copy-start.6 = (s32[1024]{0:T(1024)S(1)}, s32[1024]{0:T(1024)}, u32[]{:S(2)}) copy-start(s32[1024]{0:T(1024)} %param.14) | copy-start | bytes 12292
  47.0 6.5 %copy-start.7 = (s32[1024]{0:T(1024)S(1)}, s32[1024]{0:T(1024)}, u32[]{:S(2)}) copy-start(s32[1024]{0:T(1024)} %param.15) | copy-start | bytes 12292
  47.0 6.6 %copy-start.8 = (s32[1024]{0:T(1024)S(1)}, s32[1024]{0:T(1024)}, u32[]{:S(2)}) copy-start(s32[1024]{0:T(1024)} %param.16) | copy-start | bytes 12292
  47.0 35.3 %all-to-all-start.1 = ((bf16[64,1,32,256]{3,2,1,0:T(8,128)(2,1)}), bf16[64,1,32,256]{3,2,1,0:T(8,128)(2,1)}, u32[]{:S(2)}, u32[]{:S(2)}) async-start(bf16[64,1,32,256]{3,2,1,0:T(8,128)(2,1)} %bitcast.1), calls=%async_computation.1 | async-start | bytes 2097152 | tf_op jit(solution)/shard_map/all_to_all | solution.py:52
  86.4 2.6 copy-start.3
  86.6 2.8 copy-start
  90.4 1.7 copy-start.1
  96.1 2.6 copy-start.3
  96.4 2.8 copy-start
  100.1 1.7 copy-start.1
  105.8 2.6 copy-start.3
  106.1 2.8 copy-start
  109.8 1.7 copy-start.1
  115.6 2.6 copy-start.3
  115.8 2.8 copy-start
  119.6 1.7 copy-start.1
  121.2 7.1 %copy-start.5 = (s32[1,64,32]{2,0,1:T(1,128)S(1)}, s32[1,64,32]{2,0,1:T(1,128)}, u32[]{:S(2)}) copy-start(s32[1,64,32]{2,0,1:T(1,128)} %copy-done.4) | copy-start | bytes 24580
  121.2 7.2 %copy-start.9 = (s32[256]{0:T(256)S(1)}, s32[256]{0:T(256)}, u32[]{:S(2)}) copy-start(s32[256]{0:T(256)} %param.18) | copy-start | bytes 3076
  122.3 34.6 %all-to-all-start.2 = ((bf16[1,64,32,256]{3,2,0,1:T(8,128)(2,1)}), bf16[1,64,32,256]{3,2,0,1:T(8,128)(2,1)}, u32[]{:S(2)}, u32[]{:S(2)}) async-start(bf16[1,64,32,256]{3,2,0,1:T(8,128)(2,1)} %bitcast.124), calls=%async_computation.2 | async-start | bytes 2097152 | tf_op jit(solution)/shard_map/all_to_all | solution.py:145
  128.3 252.9 %all-reduce.2.cloned.1.call-start = ((), (), s32[]{:S(2)}) async-start(), calls=%async_computation.3 | async-start | bytes 2097152 | tf_op jit(solution)/shard_map/psum | solution.py:156
  169.4 27.3 %copy-start.2 = (f32[8,8,32,32]{2,3,0,1:T(8,128)S(1)}, f32[8,8,32,32]{2,3,0,1:T(8,128)}, u32[]{:S(2)}) copy-start(f32[8,8,32,32]{2,3,0,1:T(8,128)} %get-tuple-element.138) | copy-start | bytes 786436
  169.4 24.0 %collective-permute-start = (f32[1024,256]{1,0:T(8,128)S(1)}, f32[1024,256]{1,0:T(8,128)S(1)}, u32[]{:S(2)}, u32[]{:S(2)}) collective-permute-start(f32[1024,256]{1,0:T(8,128)S(1)} %scatter_custom_fusion), channel_id=1, source_target_pairs={{0,1},{1,0},{2,3},{3,2},{4,5},{5,4},{6,7},{7,6},{8,9},{9,8},{10,11... | collective-permute-start | bytes 3145736 | tf_op jit(solution)/shard_map/ppermute | solution.py:153
  193.5 24.7 %collective-permute-start.1 = (f32[1024,256]{1,0:T(8,128)S(1)}, f32[1024,256]{1,0:T(8,128)S(1)}, u32[]{:S(2)}, u32[]{:S(2)}) collective-permute-start(f32[1024,256]{1,0:T(8,128)S(1)} %add.65), channel_id=1, source_target_pairs={{0,2},{1,3},{2,0},{3,1},{4,6},{5,7},{6,4},{7,5},{8,10},{9,11},{10,... | collective-permute-start | bytes 3145736 | tf_op jit(solution)/shard_map/ppermute | solution.py:153
Sparse Core Ops, SparseCore 0:
  198.1 183.0 all-reduce.1
